TPU v7x, 128 devices: a whole 4x4x4 slice. The times are simulated.
128 devices in a mesh: ctx: 32 (over z, x, core), exp: 4 (over y).
Axes of the slice: x: 4, y: 4, z: 4, core: 2. Of those that a mesh axis runs over, the one named last changes fastest.
Arguments:
- queries: bfloat16 [8192, 4096], P('ctx', 'exp'), may hold values from -6 to 6
- key_rows: bfloat16 [8192, 4096], P('ctx', 'exp'), may hold values from -6 to 6
- value_rows: bfloat16 [8192, 4096], P('ctx', 'exp'), may hold values from -6 to 6
- gate_rows: bfloat16 [8192, 4096], P('ctx', 'exp'), may hold values from -6 to 6
- decay_exp: int32 [32], P('exp'), may hold values from 5 to 16
- attn_gain: float32 [4096], P('exp'), may hold values from 0.1 to 1.9
- out_proj: bfloat16 [4096, 6144], P('exp'), may hold values from -0.09375 to 0.09375
- residual: bfloat16 [8192, 6144], P(('ctx', 'exp')), may hold values from -6 to 6
- norm_gain: float32 [6144], replicated, may hold values from 0.1 to 1.9
- routes: int32 [8192, 2], P('ctx'), may hold values from 0 to 31, as said below
- route_weights: float32 [8192, 2], P('ctx'), may hold values from 0.1 to 1
- w_gate: bfloat16 [4, 9216, 6144], P('exp', 'ctx'), may hold values from -0.078125 to 0.078125
- w_up: bfloat16 [4, 9216, 6144], P('exp', 'ctx'), may hold values from -0.078125 to 0.078125
- w_down: bfloat16 [4, 9216, 6144], P('exp', 'ctx'), may hold values from -0.0625 to 0.0625
Outputs:
- layer_out: bfloat16 [8192, 6144], P(('ctx', 'exp'))
Inputs may be any that keep to these rules, and one draw needn't show every extreme that they name: `routes`: A row's two entries differ. An expert e below 4 is named only in column e % 2. In every aligned block of 64 rows each expert below 4 is named at most 8 times, and some expert below 4 exactly 8 times.
All inputs are finite; a program needn't handle non-finite values.
Results may differ from a plain program's by a relative error of at most 0.018.
Values may be sent and summed in bfloat16 or wider, within the bound.
A program may use at most 128 MiB of HBM per device.

v0:
```python
import jax
import jax.numpy as jnp
from jax import lax
from jax.sharding import PartitionSpec as P

EPSILON = 1e-06


def prefix(shard, axis, combine, identity):
    size, index = (lax.axis_size(axis), lax.axis_index(axis))
    everything = jax.tree.map(
        lambda part, kind: lax.all_gather(part.astype(kind), axis),
        shard,
        (jnp.bfloat16, jnp.bfloat16),
    )
    start = jax.tree.map(
        lambda part, zero: jnp.broadcast_to(jnp.asarray(zero, part.dtype), part.shape),
        shard,
        identity,
    )

    def turn(k, before):
        reached = k < index
        new = combine(
            before, jax.tree.map(lambda part, own: part[k].astype(own.dtype), everything, shard)
        )
        return jax.tree.map(lambda a, b: jnp.where(reached, a, b), new, before)

    return lax.fori_loop(0, size, turn, start)


def span_local(queries, key_rows, value_rows, decay_exp):
    row_count = queries.shape[0]
    head_count = decay_exp.shape[0]
    head_width = queries.shape[1] // head_count
    query_heads = queries.reshape(row_count, head_count, head_width)
    key_heads = key_rows.reshape(row_count, head_count, head_width)
    value_heads = value_rows.reshape(row_count, head_count, head_width)
    decay_rates = jnp.exp2(-decay_exp.astype(jnp.float32))
    positions = jnp.arange(row_count, dtype=jnp.float32)
    offsets = positions[:, None] - positions[None, :]
    damping = jnp.where(
        offsets[None] >= 0.0,
        jnp.exp(-decay_rates[:, None, None] * jnp.maximum(offsets, 0.0)[None]),
        0.0,
    )
    scores = jnp.einsum("thd,shd->hts", query_heads, key_heads, preferred_element_type=jnp.float32)
    mixing = (scores * damping).astype(jnp.bfloat16)
    inner_part = jnp.einsum("hts,shd->thd", mixing, value_heads, preferred_element_type=jnp.float32)
    tail_decay = jnp.exp(-decay_rates[None, :] * (row_count - 1.0 - positions)[:, None])
    keyed_rows = (key_heads.astype(jnp.float32) * tail_decay[:, :, None]).astype(jnp.bfloat16)
    update = jnp.einsum("shd,she->hde", keyed_rows, value_heads, preferred_element_type=jnp.float32)
    carry_decay = jnp.exp(-decay_rates * row_count)
    lead_decay = jnp.exp(-decay_rates[None, :] * (positions + 1.0)[:, None])
    leading = query_heads.astype(jnp.float32) * lead_decay[:, :, None]
    return (inner_part, leading, update, carry_decay)


def join_states(earlier, later):
    return (earlier[0] * later[0], later[0][:, None, None] * earlier[1] + later[1])


def settle(inner_part, leading, prior_state, gate_rows, attn_gain):
    outer_part = jnp.einsum("thd,hde->the", leading, prior_state, precision=lax.Precision.HIGHEST)
    mixed_heads = inner_part + outer_part
    row_count, head_count, head_width = mixed_heads.shape
    mean_square = jnp.mean(mixed_heads * mixed_heads, axis=2, keepdims=True)
    normed_heads = mixed_heads * lax.rsqrt(mean_square + EPSILON)
    gain_heads = attn_gain.reshape(head_count, head_width)
    gate_heads = gate_rows.reshape(row_count, head_count, head_width).astype(jnp.float32)
    settled = (normed_heads * gain_heads * jax.nn.sigmoid(gate_heads)).astype(jnp.bfloat16)
    return settled.reshape(row_count, head_count * head_width)


def token_norm(hidden, norm_gain):
    mean_square = jnp.mean(hidden * hidden, axis=1, keepdims=True)
    return (hidden * lax.rsqrt(mean_square + EPSILON) * norm_gain).astype(jnp.bfloat16)


def slot_tables(owners, chosen_ids, weights, capacity):
    column = owners % 2
    chosen = jnp.where(column[:, None] == 0, chosen_ids[None, :, 0], chosen_ids[None, :, 1])
    weight_rows = jnp.where(column[:, None] == 0, weights[None, :, 0], weights[None, :, 1])
    picked = chosen == owners[:, None]
    slot_rank = jnp.cumsum(picked.astype(jnp.int32), axis=1) - 1
    slot_ids = jnp.arange(capacity, dtype=jnp.int32)
    slot_table = picked[:, None, :] & (slot_rank[:, None, :] == slot_ids[None, :, None])
    return (slot_table.astype(jnp.bfloat16), jnp.where(slot_table, weight_rows[:, None, :], 0.0))


def expert_part(slot_rows, gate_cols, up_cols, down_rows):
    contract_dims = (((1,), (1,)), ((), ()))
    first_half = lax.dot_general(
        slot_rows, gate_cols, contract_dims, preferred_element_type=jnp.float32
    )
    second_half = lax.dot_general(
        slot_rows, up_cols, contract_dims, preferred_element_type=jnp.float32
    )
    activated = (jax.nn.silu(first_half) * second_half).astype(jnp.bfloat16)
    return jnp.dot(activated, down_rows, preferred_element_type=jnp.float32)


def body(
    queries,
    key_rows,
    value_rows,
    gate_rows,
    decay_exp,
    attn_gain,
    out_proj,
    residual,
    norm_gain,
    routes,
    route_weights,
    w_gate,
    w_up,
    w_down,
):
    inner_part, leading, update, carry_decay = span_local(queries, key_rows, value_rows, decay_exp)
    head_count = decay_exp.shape[0]
    head_width = queries.shape[1] // head_count
    identity = (
        jnp.ones((head_count,), jnp.float32),
        jnp.zeros((head_count, head_width, head_width), jnp.float32),
    )
    carried, prior_state = prefix((carry_decay, update), "ctx", join_states, identity)
    settled = settle(inner_part, leading, prior_state, gate_rows, attn_gain)
    span_rows = queries.shape[0]
    group_count = lax.axis_size("exp")
    group_rows = span_rows // group_count
    group_index = lax.axis_index("exp")
    first_mine = group_index * group_rows
    capacity = group_rows // 8
    gate_cols = w_gate[0]
    up_cols = w_up[0]
    down_rows = w_down[0]
    placed = lax.dynamic_update_slice_in_dim(
        jnp.zeros((span_rows, residual.shape[1]), jnp.float32),
        residual.astype(jnp.float32),
        first_mine,
        0,
    )
    projected = jnp.dot(settled, out_proj, preferred_element_type=jnp.float32) + placed
    hidden_all = lax.psum(projected.astype(jnp.bfloat16), "exp").astype(jnp.float32)
    normed_all = token_norm(hidden_all, norm_gain)
    owners = jnp.reshape(group_index, (1,))
    slot_table, weighted = slot_tables(owners, routes, route_weights, capacity * group_count)
    outgoing = jnp.einsum(
        "ecn,nd->cd", slot_table, normed_all, preferred_element_type=jnp.float32
    ).astype(jnp.bfloat16)
    gathered = lax.all_gather(outgoing, "ctx", axis=0, tiled=True)
    produced = lax.psum_scatter(
        expert_part(gathered, gate_cols, up_cols, down_rows).astype(jnp.bfloat16),
        "ctx",
        scatter_dimension=0,
        tiled=True,
    ).astype(jnp.float32)
    spread_back = jnp.einsum("ecn,cd->nd", weighted, produced, precision=lax.Precision.HIGHEST)
    mixture = lax.psum_scatter(
        spread_back.astype(jnp.bfloat16), "exp", scatter_dimension=0, tiled=True
    ).astype(jnp.float32)
    hidden = lax.dynamic_slice_in_dim(hidden_all, first_mine, group_rows, 0)
    return (hidden + mixture).astype(jnp.bfloat16)


def solution(mesh):
    in_specs = (
        P("ctx", "exp"),
        P("ctx", "exp"),
        P("ctx", "exp"),
        P("ctx", "exp"),
        P("exp"),
        P("exp"),
        P("exp", None),
        P(("ctx", "exp"), None),
        P(),
        P("ctx", None),
        P("ctx", None),
        P("exp", "ctx", None),
        P("exp", "ctx", None),
        P("exp", "ctx", None),
    )
    out_specs = P(("ctx", "exp"), None)
    return jax.shard_map(body, mesh=mesh, in_specs=in_specs, out_specs=out_specs, check_vma=False)
```

profile of v0, /device:TPU:1, one launch (start us, length us, event | category | flops | bytes accessed | tf_op | source)
XLA Modules:
  0.0 523.0 jit_solution(2067149946234657723)
XLA Ops:
  7.9 2.1 copy.36
  10.7 2.2 convolution_convert_fusion.3
  15.6 65.4 %all-reduce = bf16[256]{0:T(256)(128)(2,1)S(1)} all-reduce(bf16[256]{0:T(256)(128)(2,1)S(1)} %dynamic-update-slice.1), channel_id=2, replica_groups=mesh['ctx'=32,'exp'=4] {'ctx'}, use_global_device_ids=true, to_apply=%add | all-reduce | flops 256 | bytes 1024
  81.7 2.3 add_divide_fusion
  84.0 2.6 copy.34
  88.1 86.4 %while.14 = (s32[]{:T(128)}, f32[8,128,128]{2,1,0:T(8,128)}, s32[]{:T(128)}, bf16[32,8]{1,0:T(8,128)(2,1)}, bf16[32,8,128,128]{3,2,1,0:T(8,128)(2,1)}, /*index=5*/s32[]{:T(128)}, s32[]{:T(128)}) while((s32[]{:T(128)}, f32[8,128,128]{2,1,0:T(8,128)}, s32[]{:T(128)}, bf16[32,8]{1,0:T(8,128)(2,1)}, ...), condition=%wide.region_1.2_spmd.clone, body=%wide.region_0.1_spmd.clone.sunk | while | flops 655372 | bytes 1310905 | solution.py:29
  91.3 2.0 fusion.70
  94.1 2.0 fusion.70
  102.2 2.0 fusion.70
  174.5 3.6 convolution_bitcast_fusion
  178.1 3.7 multiply_reduce_fusion.1
  183.6 6.7 %fusion.57 = f32[256,6144]{1,0:T(8,128)S(1)} fusion(bf16[256,1024]{0,1:T(8,128)(2,1)S(1)} %bitcast.89, bf16[1024,6144]{1,0:T(8,128)(2,1)} %param.22), kind=kOutput, calls=%fused_computation.78 | convolution fusion | flops 3221225472 | bytes 19398656 | tf_op jit(solution)/shard_map/dot_general | solution.py:143
  190.6 2.1 convert_element_type.110
  193.5 76.0 %all-reduce.3.cloned.1.call-done = bf16[256,6144]{1,0:T(8,128)(2,1)} async-done(((bf16[256,6144]{1,0:T(8,128)(2,1)}), bf16[256,6144]{1,0:T(8,128)(2,1)}) %all-reduce.3.cloned.1.call-update) | async-done | bytes 3145744 | tf_op jit(solution)/shard_map/psum | solution.py:144
  269.6 2.6 multiply_reduce_fusion
  272.2 3.7 convolution_convert_fusion.2
  276.1 63.1 %all-gather.5.cloned.1.call-done = bf16[1024,6144]{1,0:T(8,128)(2,1)} async-done(((bf16[32,6144]{1,0:T(8,128)(2,1)}), bf16[1024,6144]{1,0:T(8,128)(2,1)}) %all-gather.5.cloned.1.call-update) | async-done | bytes 12582928 | tf_op jit(solution)/shard_map/all_gather | solution.py:151
  339.2 10.5 %fusion.4 = f32[1024,288]{0,1:T(8,128)} fusion(bf16[1024,6144]{1,0:T(8,128)(2,1)} %all-gather.5.cloned.1.call-done, bf16[1,288,6144]{2,1,0:T(8,128)(2,1)} %param.27), kind=kOutput, calls=%fused_computation.11 | convolution fusion | flops 3623878656 | bytes 17301504 | tf_op jit(solution)/shard_map/dot_general | solution.py:93
  349.7 17.7 %convolution_convert_fusion = bf16[1024,6144]{1,0:T(8,128)(2,1)} fusion(bf16[1,288,6144]{2,1,0:T(8,128)(2,1)S(1)} %copy-done, bf16[1024,6144]{1,0:T(8,128)(2,1)} %all-gather.5.cloned.1.call-done, bf16[1,288,6144]{2,1,0:T(8,128)(2,1)} %param.28, f32[1024,288]{0,1:T(8,128)} %fusion.4), kind=kOutput, calls=%fused_computation.3 | convolution fusion | flops 7255818240 | bytes 33423360 | tf_op jit(solution)/shard_map/dot_general | solution.py:100
  368.0 101.9 %reduce-scatter.3.cloned.1.call-done = bf16[32,6144]{1,0:T(8,128)(2,1)} async-done(((bf16[1024,6144]{1,0:T(8,128)(2,1)}), bf16[32,6144]{1,0:T(8,128)(2,1)}) %reduce-scatter.3.cloned.1.call-update) | async-done | bytes 393232 | tf_op jit(solution)/shard_map/reduce_scatter | solution.py:152
  469.9 5.1 convolution_convert_fusion.1
  475.1 5.4 %convert_element_type.111 = f32[256,6144]{1,0:T(8,128)} convert(bf16[256,6144]{1,0:T(8,128)(2,1)} %all-reduce.3.cloned.1.call-done) | non-fusion elementwise | flops 1572864 | bytes 9437184 | tf_op jit(solution)/shard_map/convert_element_type | solution.py:144
  480.5 33.3 %reduce-scatter.5.cloned.1.call-done = bf16[64,6144]{1,0:T(8,128)(2,1)} async-done(((bf16[256,6144]{1,0:T(8,128)(2,1)}), bf16[64,6144]{1,0:T(8,128)(2,1)}) %reduce-scatter.5.cloned.1.call-update) | async-done | bytes 786448 | tf_op jit(solution)/shard_map/reduce_scatter | solution.py:159
  513.8 2.7 add_convert_fusion
  (109 shorter events, 90.5 us)
Async XLA Ops:
  6.5 343.1 %copy-start = (bf16[1,288,6144]{2,1,0:T(8,128)(2,1)S(1)}, bf16[1,288,6144]{2,1,0:T(8,128)(2,1)}, u32[]{:S(2)}) copy-start(bf16[1,288,6144]{2,1,0:T(8,128)(2,1)} %param.29) | copy-start | bytes 10616836
  6.5 81.6 %all-gather.7.cloned.1.call-start = ((), (), s32[]{:S(2)}) async-start(), calls=%async_computation.6 | async-start | bytes 8650752 | tf_op jit(solution)/shard_map/all_gather | solution.py:12
  12.9 256.7 %all-reduce.3.cloned.1.call-start = ((), (), s32[]{:S(2)}) async-start(), calls=%async_computation.2 | async-start | bytes 6291456 | tf_op jit(solution)/shard_map/psum | solution.py:144
  88.1 90.0 %copy-start.6 = (f32[8]{0:T(128)S(1)}, f32[8]{0:T(128)}, u32[]{:S(2)}) copy-start(f32[8]{0:T(128)} %get-tuple-element.131) | copy-start | bytes 100
  174.5 7.3 %copy-start.3 = (f32[1024]{0:T(1024)S(1)}, f32[1024]{0:T(1024)}, u32[]{:S(2)}) copy-start(f32[1024]{0:T(1024)} %param.21) | copy-start | bytes 12292
  183.6 6.7 %copy-start.2 = (bf16[64,6144]{1,0:T(8,128)(2,1)S(1)}, bf16[64,6144]{1,0:T(8,128)(2,1)}, u32[]{:S(2)}) copy-start(bf16[64,6144]{1,0:T(8,128)(2,1)} %param.23) | copy-start | bytes 2359300
  190.6 2.2 copy-start.5
  192.7 146.5 %all-gather.5.cloned.1.call-start = ((), (), s32[]{:S(2)}) async-start(), calls=%async_computation.3 | async-start | bytes 12976128 | tf_op jit(solution)/shard_map/all_gather | solution.py:151
  275.9 194.0 %reduce-scatter.3.cloned.1.call-start = ((), (), s32[]{:S(2)}) async-start(), calls=%async_computation.4 | async-start | bytes 12976128 | tf_op jit(solution)/shard_map/reduce_scatter | solution.py:152
  367.3 0.7 copy-start.4
  367.4 146.5 %reduce-scatter.5.cloned.1.call-start = ((), (), s32[]{:S(2)}) async-start(), calls=%async_computation.5 | async-start | bytes 3932160 | tf_op jit(solution)/shard_map/reduce_scatter | solution.py:159
  475.0 41.5 %copy-start.1 = (bf16[1,288,6144]{2,1,0:T(8,128)(2,1)S(1)}, bf16[1,288,6144]{2,1,0:T(8,128)(2,1)}, u32[]{:S(2)}) copy-start(bf16[1,288,6144]{2,1,0:T(8,128)(2,1)} %param.29) | copy-start | bytes 10616836
Sparse Core Ops, SparseCore 0:
  13.0 56.8 all-gather.6
  192.8 76.7 all-reduce.2
  276.0 63.1 all-gather.4
  367.5 102.3 reduce-scatter.2
  475.2 38.6 reduce-scatter.4
where the time goes:
time: 525 us; the launch traced here: 523 us
  waiting for transfers between devices  274 us (52%)
  other arithmetic  108 us (21%)
  blocking collectives  65.4 us (12%)
  matrix products  53 us (10%)
  between operations  13.8 us (3%)
  local copies, waits for them, and re-layouts  8.36 us (2%)
    reduce_scatter x1, waiting for transfers between devices, body(): lax.psum_scatter(expert_part(gathered, gate_cols, up_cols, down_rows).ast...  102 us
    psum x1, waiting for transfers between devices, body(): lax.psum(projected.astype(jnp.bfloat16), 'exp').astype(jnp.float32)  76 us
    unnamed x1, blocking collectives  65.4 us
    select_n x32, other arithmetic, turn(): return jax.tree.map(lambda a, b: jnp.where(reached, a, b), new, before)  65.1 us
    all_gather x1, waiting for transfers between devices, body(): gathered = lax.all_gather(outgoing, 'ctx', axis=0, tiled=True)  63.1 us
    reduce_scatter x1, waiting for transfers between devices, body(): lax.psum_scatter(spread_back.astype(jnp.bfloat16), 'exp', scatter_dimensi...  33.3 us
    convert_element_type x32, other arithmetic, turn(): part[k].astype(own.dtype)  21.3 us
    dot_general x1, matrix products, expert_part(): return jnp.dot(activated, down_rows, preferred_element_type=jnp.float32)  17.7 us
  transfers between devices with their start and end apart: 5, of which 4 were waited for; matrix products, arithmetic and copies ran while one was open for 3% of the time, Pallas kernels for 0%

commit v1 on v0

--- a/solution.py
+++ b/solution.py
@@ -4,6 +4,13 @@
 from jax.sharding import PartitionSpec as P
 
 EPSILON = 1e-06
+
+
+def exchange_gather(x, axis, d):
+    devices = lax.axis_size(axis)
+    blocks = jnp.stack([x for _ in range(devices)])
+    blocks = lax.all_to_all(blocks, axis, split_axis=0, concat_axis=0)
+    return jnp.concatenate(blocks, axis=d)
 
 
 def prefix(shard, axis, combine, identity):
@@ -148,7 +155,7 @@
     outgoing = jnp.einsum(
         "ecn,nd->cd", slot_table, normed_all, preferred_element_type=jnp.float32
     ).astype(jnp.bfloat16)
-    gathered = lax.all_gather(outgoing, "ctx", axis=0, tiled=True)
+    gathered = exchange_gather(outgoing, "ctx", 0)
     produced = lax.psum_scatter(
         expert_part(gathered, gate_cols, up_cols, down_rows).astype(jnp.bfloat16),
         "ctx",

time: 525 us -> 614 us (1.17)
  blocking collectives: 65.4 us -> 214 us
  waiting for transfers between devices: 274 us -> 211 us
  local copies, waits for them, and re-layouts: 8.36 us -> 19 us
  matrix products: 53 us -> 46.7 us
    all_to_all x0 -> x1, blocking collectives: none -> 149 us  [exchange_gather(): blocks = lax.all_to_all(blocks, axis, split_axis=0, concat_axis=0)]
    all_gather x1 -> x0, waiting for transfers between devices: 63.1 us -> none  [body(): gathered = lax.all_gather(outgoing, 'ctx', axis=0, tiled=True)]
    another operation x2 -> x3, local copies, waits for them, and re-layouts: 0.08 us -> 6.22 us  [the longest x1 6.14 us: exchange_gather(): blocks = jnp.stack([x for _ in range(devices)])]
  transfers between devices with their start and end apart: 5 -> 4, of which waited for: 4 -> 3; matrix products, arithmetic and copies ran while one was open for 3% -> 2% of each run, Pallas kernels for 0% -> 0%
where the time goes in v1:
time: 614 us; the launch traced here: 612 us
  blocking collectives  214 us (35%)
  waiting for transfers between devices  211 us (34%)
  other arithmetic  107 us (17%)
  matrix products  46.7 us (8%)
  local copies, waits for them, and re-layouts  19 us (3%)
  between operations  13.8 us (2%)
    all_to_all x1, blocking collectives, exchange_gather(): blocks = lax.all_to_all(blocks, axis, split_axis=0, concat_axis=0)  149 us
    reduce_scatter x1, waiting for transfers between devices, body(): lax.psum_scatter(expert_part(gathered, gate_cols, up_cols, down_rows).ast...  101 us
    psum x1, waiting for transfers between devices, body(): lax.psum(projected.astype(jnp.bfloat16), 'exp').astype(jnp.float32)  76 us
    unnamed x1, blocking collectives  65.4 us
    select_n x32, other arithmetic, turn(): return jax.tree.map(lambda a, b: jnp.where(reached, a, b), new, before)  65.1 us
    reduce_scatter x1, waiting for transfers between devices, body(): lax.psum_scatter(spread_back.astype(jnp.bfloat16), 'exp', scatter_dimensi...  33.5 us
    convert_element_type x32, other arithmetic, turn(): part[k].astype(own.dtype)  21.3 us
    dot_general x1, matrix products, expert_part(): return jnp.dot(activated, down_rows, preferred_element_type=jnp.float32)  17.6 us
  transfers between devices with their start and end apart: 4, of which 3 were waited for; matrix products, arithmetic and copies ran while one was open for 2% of the time, Pallas kernels for 0%

profile of v1, /device:TPU:1, one launch (start us, length us, event | category | flops | bytes accessed | tf_op | source)
XLA Modules:
  0.0 611.9 jit_solution(1556892502988688035)
XLA Ops:
  7.9 2.1 copy.36
  10.7 2.2 convolution_convert_fusion.3
  15.6 65.4 %all-reduce = bf16[256]{0:T(256)(128)(2,1)S(1)} all-reduce(bf16[256]{0:T(256)(128)(2,1)S(1)} %dynamic-update-slice.1), channel_id=2, replica_groups=mesh['ctx'=32,'exp'=4] {'ctx'}, use_global_device_ids=true, to_apply=%add | all-reduce | flops 256 | bytes 1024
  81.7 2.3 add_divide_fusion
  84.0 2.6 copy.34
  88.1 86.4 %while.14 = (s32[]{:T(128)}, f32[8,128,128]{2,1,0:T(8,128)}, s32[]{:T(128)}, bf16[32,8]{1,0:T(8,128)(2,1)}, bf16[32,8,128,128]{3,2,1,0:T(8,128)(2,1)}, /*index=5*/s32[]{:T(128)}, s32[]{:T(128)}) while((s32[]{:T(128)}, f32[8,128,128]{2,1,0:T(8,128)}, s32[]{:T(128)}, bf16[32,8]{1,0:T(8,128)(2,1)}, ...), condition=%wide.region_1.2_spmd.clone, body=%wide.region_0.1_spmd.clone.sunk | while | flops 655372 | bytes 1310905 | solution.py:36
  102.2 2.0 fusion.70
  174.5 3.6 convolution_bitcast_fusion
  178.1 3.7 multiply_reduce_fusion.1
  183.6 6.7 %fusion.57 = f32[256,6144]{1,0:T(8,128)S(1)} fusion(bf16[256,1024]{0,1:T(8,128)(2,1)S(1)} %bitcast.92, bf16[1024,6144]{1,0:T(8,128)(2,1)} %param.22), kind=kOutput, calls=%fused_computation.78 | convolution fusion | flops 3221225472 | bytes 19398656 | tf_op jit(solution)/shard_map/dot_general | solution.py:150
  190.6 2.1 convert_element_type.110
  193.5 76.0 %all-reduce.3.cloned.1.call-done = bf16[256,6144]{1,0:T(8,128)(2,1)} async-done(((bf16[256,6144]{1,0:T(8,128)(2,1)}), bf16[256,6144]{1,0:T(8,128)(2,1)}) %all-reduce.3.cloned.1.call-update) | async-done | bytes 3145744 | tf_op jit(solution)/shard_map/psum | solution.py:151
  269.6 2.6 multiply_reduce_fusion
  272.2 2.9 convolution_convert_fusion.2
  275.1 6.1 %stack.2 = bf16[32,32,6144]{2,1,0:T(8,128)(2,1)} broadcast(bf16[32,6144]{1,0:T(8,128)(2,1)S(1)} %convolution_convert_fusion.2), dimensions={1,2} | broadcast | bytes 12976128 | tf_op jit(solution)/shard_map/stack | solution.py:11
  281.2 148.7 %all_to_all.5 = bf16[32,32,6144]{2,1,0:T(8,128)(2,1)S(1)} all-to-all(bf16[32,32,6144]{2,1,0:T(8,128)(2,1)} %stack.2), channel_id=1, replica_groups=mesh['ctx'=32,'exp'=4] {'ctx'}, dimensions={0} | all-to-all | bytes 25165824 | tf_op jit(solution)/shard_map/all_to_all | solution.py:12
  429.9 4.5 copy-done.1
  434.4 4.9 fusion.4
  439.3 17.6 %convolution_convert_fusion = bf16[1024,6144]{1,0:T(8,128)(2,1)} fusion(bf16[1,288,6144]{2,1,0:T(8,128)(2,1)S(1)} %copy-done, bf16[1024,6144]{1,0:T(8,128)(2,1)} %bitcast.90, bf16[1,288,6144]{2,1,0:T(8,128)(2,1)} %param.28, f32[1024,288]{0,1:T(8,128)} %fusion.4), kind=kOutput, calls=%fused_computation.3 | convolution fusion | flops 7255818240 | bytes 33423360 | tf_op jit(solution)/shard_map/dot_general | solution.py:107
  457.7 101.1 %reduce-scatter.3.cloned.1.call-done = bf16[32,6144]{1,0:T(8,128)(2,1)} async-done(((bf16[1024,6144]{1,0:T(8,128)(2,1)}), bf16[32,6144]{1,0:T(8,128)(2,1)}) %reduce-scatter.3.cloned.1.call-update) | async-done | bytes 393232 | tf_op jit(solution)/shard_map/reduce_scatter | solution.py:159
  558.8 5.1 convolution_convert_fusion.1
  563.9 5.3 convert_element_type.111
  569.2 33.5 %reduce-scatter.5.cloned.1.call-done = bf16[64,6144]{1,0:T(8,128)(2,1)} async-done(((bf16[256,6144]{1,0:T(8,128)(2,1)}), bf16[64,6144]{1,0:T(8,128)(2,1)}) %reduce-scatter.5.cloned.1.call-update) | async-done | bytes 786448 | tf_op jit(solution)/shard_map/reduce_scatter | solution.py:166
  602.7 2.7 add_convert_fusion
  (110 shorter events, 94.3 us)
Async XLA Ops:
  6.5 432.8 %copy-start = (bf16[1,288,6144]{2,1,0:T(8,128)(2,1)S(1)}, bf16[1,288,6144]{2,1,0:T(8,128)(2,1)}, u32[]{:S(2)}) copy-start(bf16[1,288,6144]{2,1,0:T(8,128)(2,1)} %param.29) | copy-start | bytes 10616836
  6.5 81.6 %all-gather.4.cloned.1.call-start = ((), (), s32[]{:S(2)}) async-start(), calls=%async_computation.6 | async-start | bytes 8650752 | tf_op jit(solution)/shard_map/all_gather | solution.py:19
  12.9 256.7 %all-reduce.3.cloned.1.call-start = ((), (), s32[]{:S(2)}) async-start(), calls=%async_computation.3 | async-start | bytes 6291456 | tf_op jit(solution)/shard_map/psum | solution.py:151
  88.1 90.0 %copy-start.6 = (f32[8]{0:T(128)S(1)}, f32[8]{0:T(128)}, u32[]{:S(2)}) copy-start(f32[8]{0:T(128)} %get-tuple-element.131) | copy-start | bytes 100
  174.5 7.3 %copy-start.3 = (f32[1024]{0:T(1024)S(1)}, f32[1024]{0:T(1024)}, u32[]{:S(2)}) copy-start(f32[1024]{0:T(1024)} %param.21) | copy-start | bytes 12292
  183.6 6.7 %copy-start.2 = (bf16[64,6144]{1,0:T(8,128)(2,1)S(1)}, bf16[64,6144]{1,0:T(8,128)(2,1)}, u32[]{:S(2)}) copy-start(bf16[64,6144]{1,0:T(8,128)(2,1)} %param.23) | copy-start | bytes 2359300
  190.6 2.2 copy-start.5
  192.7 366.1 %reduce-scatter.3.cloned.1.call-start = ((), (), s32[]{:S(2)}) async-start(), calls=%async_computation.4 | async-start | bytes 12976128 | tf_op jit(solution)/shard_map/reduce_scatter | solution.py:159
  281.2 153.2 %copy-start.7 = (bf16[1,288,6144]{2,1,0:T(8,128)(2,1)S(1)}, bf16[1,288,6144]{2,1,0:T(8,128)(2,1)}, u32[]{:S(2)}) copy-start(bf16[1,288,6144]{2,1,0:T(8,128)(2,1)} %param.27) | copy-start | bytes 10616836
  429.9 4.5 copy-start.1
  457.0 0.7 copy-start.4
  457.0 145.7 %reduce-scatter.5.cloned.1.call-start = ((), (), s32[]{:S(2)}) async-start(), calls=%async_computation.5 | async-start | bytes 3932160 | tf_op jit(solution)/shard_map/reduce_scatter | solution.py:166
Sparse Core Ops, SparseCore 0:
  13.0 56.8 all-gather.3
  192.8 76.7 all-reduce.2
  457.1 101.5 reduce-scatter.2
  564.0 38.5 reduce-scatter.4
